TPU v7x, 32 devices: a whole 2x2x4 slice. The times are simulated.
32 devices in a mesh: ctx: 16 (over z, x, core), chan: 2 (over y).
Axes of the slice: x: 2, y: 2, z: 4, core: 2. Of those that a mesh axis runs over, the one named last changes fastest.
Arguments:
- query_act: bfloat16 [2048, 1024], P('ctx', 'chan'), may hold values from -6 to 6
- key_act: bfloat16 [2048, 1024], P('ctx', 'chan'), may hold values from -6 to 6
- value_act: bfloat16 [2048, 1024], P('ctx', 'chan'), may hold values from -6 to 6
- filters: bfloat16 [2048, 1024], P('ctx', 'chan'), may hold values from -0.125 to 0.125
- skip_scale: float32 [1024], P('chan'), may hold values from -4 to 4
- w_out: bfloat16 [1024, 4096], P('chan'), may hold values from -0.25 to 0.25
Outputs:
- projected: bfloat16 [2048, 4096], P('ctx', 'chan')
All inputs are finite; a program needn't handle non-finite values.
Results may differ from a plain program's by a relative error of at most 0.015.
Values may be sent and summed in bfloat16 or wider, within the bound.
A program may use at most 64 MiB of HBM per device.

v0:
```python
import math
import jax
import jax.numpy as jnp
from jax import lax
from jax.sharding import PartitionSpec as P

precise = lax.Precision.HIGHEST


def phase_table(row_count, col_count, modulus, factor):
    row_index = lax.broadcasted_iota(jnp.int32, (row_count, col_count), 0)
    col_index = lax.broadcasted_iota(jnp.int32, (row_count, col_count), 1)
    phase_angle = (row_index * col_index % modulus).astype(jnp.float32) * (2.0 * math.pi / modulus)
    return (jnp.cos(phase_angle) * factor, jnp.sin(phase_angle) * factor)


def twiddle(freq_index, pos_index, modulus):
    phase_angle = (freq_index * pos_index % modulus).astype(jnp.float32) * (2.0 * math.pi / modulus)
    return (jnp.cos(phase_angle), jnp.sin(phase_angle))


def shards(query_act, key_act, value_act, filters, skip_scale, w_out):
    tok_rows, chan_width = key_act.shape
    ctx_size = lax.axis_size("ctx")
    per_dev = tok_rows // ctx_size
    fft_length = 2 * tok_rows * ctx_size
    freq_blocks = 2 * ctx_size
    ctx_index = lax.axis_index("ctx")
    gated_in = (key_act.astype(jnp.float32) * value_act.astype(jnp.float32)).astype(jnp.bfloat16)
    sent_input, sent_filter = (
        lax.all_to_all(
            gated_in.reshape(1, ctx_size, per_dev, chan_width),
            "ctx",
            split_axis=1,
            concat_axis=0,
            tiled=True,
        ),
        lax.all_to_all(
            filters.reshape(1, ctx_size, per_dev, chan_width),
            "ctx",
            split_axis=1,
            concat_axis=0,
            tiled=True,
        ),
    )
    block_cos, block_sin = phase_table(freq_blocks, ctx_size, freq_blocks, 1.0)
    offsets = ctx_index * per_dev + lax.broadcasted_iota(jnp.int32, (1, per_dev), 1)
    all_freq = lax.broadcasted_iota(jnp.int32, (freq_blocks, 1), 0)
    front_cos, front_sin = twiddle(all_freq, offsets, fft_length)
    front_cos = front_cos[:, :, None]
    front_sin = front_sin[:, :, None]

    def first_section(signal):
        values32 = signal.reshape(ctx_size, per_dev, chan_width).astype(jnp.float32)
        real_part = jnp.einsum("kp,pjc->kjc", block_cos, values32, precision=precise)
        imag_part = -jnp.einsum("kp,pjc->kjc", block_sin, values32, precision=precise)
        out_real = real_part * front_cos + imag_part * front_sin
        out_imag = imag_part * front_cos - real_part * front_sin
        return jnp.stack([out_real, out_imag]).reshape(2, ctx_size, 2, per_dev, chan_width)

    cycle_cos, cycle_sin = phase_table(tok_rows, tok_rows, tok_rows, 1.0)

    def cycle_apply(table, operand):
        return jnp.einsum("kn,zmnc->zmkc", table, operand, precision=precise)

    spec_input = lax.all_to_all(
        first_section(sent_input), "ctx", split_axis=1, concat_axis=3, tiled=True
    )
    spec_filter = lax.all_to_all(
        first_section(sent_filter), "ctx", split_axis=1, concat_axis=3, tiled=True
    )

    def forward(portion):
        real_in = portion[0]
        imag_in = portion[1]
        out_real = cycle_apply(cycle_cos, real_in) + cycle_apply(cycle_sin, imag_in)
        out_imag = cycle_apply(cycle_cos, imag_in) - cycle_apply(cycle_sin, real_in)
        return (out_real, out_imag)

    input_real, input_imag = forward(spec_input)
    filter_real, filter_imag = forward(spec_filter)
    prod_real = input_real * filter_real - input_imag * filter_imag
    prod_imag = input_real * filter_imag + input_imag * filter_real
    back_real = cycle_apply(cycle_cos, prod_real) - cycle_apply(cycle_sin, prod_imag)
    back_imag = cycle_apply(cycle_cos, prod_imag) + cycle_apply(cycle_sin, prod_real)
    mixed = jnp.stack([back_real, back_imag])
    inverted = mixed[:, 0]
    pack_width = inverted.shape[-1]
    own_freq = 2 * ctx_index + lax.broadcasted_iota(jnp.int32, (2, 1), 0)
    all_offsets = lax.broadcasted_iota(jnp.int32, (1, tok_rows), 1)
    back_cos, back_sin = twiddle(own_freq, all_offsets, fft_length)
    back_cos = back_cos[:, :, None]
    back_sin = back_sin[:, :, None]
    turned_real = inverted[0] * back_cos - inverted[1] * back_sin
    turned_imag = inverted[0] * back_sin + inverted[1] * back_cos
    turned = jnp.stack([turned_real, turned_imag]).reshape(2, 2, ctx_size, per_dev, pack_width)
    last_cos, last_sin = phase_table(ctx_size, freq_blocks, freq_blocks, 1.0 / fft_length)

    def last_apply(table, operand):
        return jnp.einsum("nk,kzmc->nzmc", table, operand, precision=precise)

    portion = lax.all_to_all(turned, "ctx", split_axis=2, concat_axis=1, tiled=True)
    returned = last_apply(last_cos, portion[0]) - last_apply(last_sin, portion[1])
    convolved = lax.all_to_all(returned, "ctx", split_axis=0, concat_axis=1, tiled=True).reshape(
        tok_rows, chan_width
    )
    gated = (
        query_act.astype(jnp.float32)
        * (convolved + skip_scale[None, :] * gated_in.astype(jnp.float32))
    ).astype(jnp.bfloat16)
    summed = lax.psum_scatter(
        lax.dot_general(
            w_out, gated, (((0,), (1,)), ((), ())), preferred_element_type=jnp.float32
        ).astype(jnp.bfloat16),
        "chan",
        scatter_dimension=0,
        tiled=True,
    )
    return summed.T


def solution(mesh):
    return jax.shard_map(
        shards,
        mesh=mesh,
        in_specs=(
            P("ctx", "chan"),
            P("ctx", "chan"),
            P("ctx", "chan"),
            P("ctx", "chan"),
            P("chan"),
            P("chan", None),
        ),
        out_specs=P("ctx", "chan"),
        check_vma=False,
    )
```

profile of v0, /device:TPU:0, one launch (start us, length us, event | category | flops | bytes accessed | tf_op | source)
XLA Modules:
  0.0 180.7 jit_solution(6431051070737040364)
XLA Ops:
  6.5 1.7 fusion.49
  8.2 7.4 %all-to-all-start = ((bf16[1,16,8,512]{3,2,0,1:T(8,128)(2,1)}), bf16[1,16,8,512]{3,2,0,1:T(8,128)(2,1)S(1)}, u32[]{:S(2)}, u32[]{:S(2)}) async-start(bf16[1,16,8,512]{3,2,0,1:T(8,128)(2,1)} %fusion.49), calls=%async_computation | async-start | bytes 262144 | tf_op jit(solution)/shard_map/all_to_all | solution.py:31
  15.7 7.8 %all-to-all-done = bf16[1,16,8,512]{3,2,0,1:T(8,128)(2,1)S(1)} async-done(((bf16[1,16,8,512]{3,2,0,1:T(8,128)(2,1)}), bf16[1,16,8,512]{3,2,0,1:T(8,128)(2,1)S(1)}, u32[]{:S(2)}, u32[]{:S(2)}) %all-to-all-start) | async-done | bytes 131104 | tf_op jit(solution)/shard_map/all_to_all | solution.py:31
  23.5 3.5 %all-to-all-start.2 = ((bf16[1,16,8,512]{3,2,0,1:T(8,128)(2,1)}), bf16[1,16,8,512]{3,2,0,1:T(8,128)(2,1)S(1)}, u32[]{:S(2)}, u32[]{:S(2)}) async-start(bf16[1,16,8,512]{3,2,0,1:T(8,128)(2,1)} %bitcast.166), calls=%async_computation.2 | async-start | bytes 262144 | tf_op jit(solution)/shard_map/all_to_all | solution.py:38
  27.0 0.5 convolution_negate_fusion.1
  27.5 0.5 fusion.24
  28.0 6.9 %all-to-all-done.2 = bf16[1,16,8,512]{3,2,0,1:T(8,128)(2,1)S(1)} async-done(((bf16[1,16,8,512]{3,2,0,1:T(8,128)(2,1)}), bf16[1,16,8,512]{3,2,0,1:T(8,128)(2,1)S(1)}, u32[]{:S(2)}, u32[]{:S(2)}) %all-to-all-start.2) | async-done | bytes 131104 | tf_op jit(solution)/shard_map/all_to_all | solution.py:38
  35.4 0.6 multiply_add_fusion.1
  36.7 1.1 pad_maximum_fusion.1
  37.8 3.7 %all-to-all-start.3 = ((f32[2,16,2,8,512]{4,3,2,0,1:T(8,128)}), f32[2,16,2,8,512]{4,3,2,0,1:T(8,128)S(1)}, u32[]{:S(2)}, u32[]{:S(2)}) async-start(f32[2,16,2,8,512]{4,3,2,0,1:T(8,128)} %pad_maximum_fusion.1), calls=%async_computation.3 | async-start | bytes 2097152 | tf_op jit(solution)/shard_map/all_to_all | solution.py:69
  42.1 1.1 pad_maximum_fusion
  43.1 21.2 %all-to-all-done.3 = f32[2,16,2,8,512]{4,3,2,0,1:T(8,128)S(1)} async-done(((f32[2,16,2,8,512]{4,3,2,0,1:T(8,128)}), f32[2,16,2,8,512]{4,3,2,0,1:T(8,128)S(1)}, u32[]{:S(2)}, u32[]{:S(2)}) %all-to-all-start.3) | async-done | bytes 1048608 | tf_op jit(solution)/shard_map/all_to_all | solution.py:69
  64.3 6.8 %all-to-all-start.1 = ((f32[2,16,2,8,512]{4,3,2,0,1:T(8,128)}), f32[2,16,2,8,512]{4,3,2,0,1:T(8,128)S(1)}, u32[]{:S(2)}, u32[]{:S(2)}) async-start(f32[2,16,2,8,512]{4,3,2,0,1:T(8,128)} %pad_maximum_fusion), calls=%async_computation.1 | async-start | bytes 2097152 | tf_op jit(solution)/shard_map/all_to_all | solution.py:66
  71.6 1.1 fusion.16
  72.7 1.1 fusion.15
  73.8 20.2 %all-to-all-done.1 = f32[2,16,2,8,512]{4,3,2,0,1:T(8,128)S(1)} async-done(((f32[2,16,2,8,512]{4,3,2,0,1:T(8,128)}), f32[2,16,2,8,512]{4,3,2,0,1:T(8,128)S(1)}, u32[]{:S(2)}, u32[]{:S(2)}) %all-to-all-start.1) | async-done | bytes 1048608 | tf_op jit(solution)/shard_map/all_to_all | solution.py:66
  94.2 1.1 fusion.14
  95.3 1.1 fusion.13
  96.4 1.1 convolution_subtract_fusion.1
  97.5 1.1 convolution_add_fusion.1
  98.7 1.1 convolution_add_fusion.2
  99.8 1.1 multiply_subtract_fusion
  100.9 0.9 fusion.8
  101.8 0.9 fusion.10
  102.7 0.9 fusion.1
  103.6 1.2 subtract_bitcast_fusion
  105.1 31.8 %all_to_all.72 = f32[2,2,16,8,512]{4,3,1,0,2:T(8,128)S(1)} all-to-all(f32[2,2,16,8,512]{4,3,1,0,2:T(8,128)S(1)} %copy.81), channel_id=1, replica_groups=mesh['ctx'=16,'chan'=2] {'ctx'}, dimensions={2} | all-to-all | bytes 2097152 | tf_op jit(solution)/shard_map/all_to_all | solution.py:102
  136.9 0.7 fusion.5
  137.6 0.7 fusion.3
  138.5 14.8 %all_to_all.73 = f32[16,1,8,512]{3,2,1,0:T(8,128)S(1)} all-to-all(f32[16,1,8,512]{3,2,1,0:T(8,128)S(1)} %copy.64), channel_id=1, replica_groups=mesh['ctx'=16,'chan'=2] {'ctx'}, dimensions={0} | all-to-all | bytes 524288 | tf_op jit(solution)/shard_map/all_to_all | solution.py:104
  153.3 1.7 fusion
  155.1 18.8 %reduce-scatter.2.cloned.1.call-done = bf16[2048,128]{0,1:T(8,128)(2,1)} async-done(((bf16[4096,128]{0,1:T(8,128)(2,1)}), bf16[2048,128]{0,1:T(8,128)(2,1)}) %reduce-scatter.2.cloned.1.call-update) | async-done | bytes 524304 | tf_op jit(solution)/shard_map/reduce_scatter | solution.py:111
  (27 shorter events, 2.8 us)
Async XLA Ops:
  8.2 15.3 %all-to-all-start = ((bf16[1,16,8,512]{3,2,0,1:T(8,128)(2,1)}), bf16[1,16,8,512]{3,2,0,1:T(8,128)(2,1)S(1)}, u32[]{:S(2)}, u32[]{:S(2)}) async-start(bf16[1,16,8,512]{3,2,0,1:T(8,128)(2,1)} %fusion.49), calls=%async_computation | async-start | bytes 262144 | tf_op jit(solution)/shard_map/all_to_all | solution.py:31
  23.5 11.4 %all-to-all-start.2 = ((bf16[1,16,8,512]{3,2,0,1:T(8,128)(2,1)}), bf16[1,16,8,512]{3,2,0,1:T(8,128)(2,1)S(1)}, u32[]{:S(2)}, u32[]{:S(2)}) async-start(bf16[1,16,8,512]{3,2,0,1:T(8,128)(2,1)} %bitcast.166), calls=%async_computation.2 | async-start | bytes 262144 | tf_op jit(solution)/shard_map/all_to_all | solution.py:38
  37.8 26.6 %all-to-all-start.3 = ((f32[2,16,2,8,512]{4,3,2,0,1:T(8,128)}), f32[2,16,2,8,512]{4,3,2,0,1:T(8,128)S(1)}, u32[]{:S(2)}, u32[]{:S(2)}) async-start(f32[2,16,2,8,512]{4,3,2,0,1:T(8,128)} %pad_maximum_fusion.1), calls=%async_computation.3 | async-start | bytes 2097152 | tf_op jit(solution)/shard_map/all_to_all | solution.py:69
  64.3 29.8 %all-to-all-start.1 = ((f32[2,16,2,8,512]{4,3,2,0,1:T(8,128)}), f32[2,16,2,8,512]{4,3,2,0,1:T(8,128)S(1)}, u32[]{:S(2)}, u32[]{:S(2)}) async-start(f32[2,16,2,8,512]{4,3,2,0,1:T(8,128)} %pad_maximum_fusion), calls=%async_computation.1 | async-start | bytes 2097152 | tf_op jit(solution)/shard_map/all_to_all | solution.py:66
  71.1 102.7 %reduce-scatter.2.cloned.1.call-start = ((), (), s32[]{:S(2)}) async-start(), calls=%async_computation.7 | async-start | bytes 1572864 | tf_op jit(solution)/shard_map/reduce_scatter | solution.py:111
  104.9 48.4 %copy-start = (bf16[512,4096]{1,0:T(8,128)(2,1)S(1)}, bf16[512,4096]{1,0:T(8,128)(2,1)}, u32[]{:S(2)}) copy-start(bf16[512,4096]{1,0:T(8,128)(2,1)} %param.11) | copy-start | bytes 12582916
  104.9 48.4 %copy-start.1 = (bf16[128,512]{1,0:T(8,128)(2,1)S(1)}, bf16[128,512]{1,0:T(8,128)(2,1)}, u32[]{:S(2)}) copy-start(bf16[128,512]{1,0:T(8,128)(2,1)} %param.8) | copy-start | bytes 393220
  104.9 48.4 %copy-start.2 = (bf16[128,512]{1,0:T(8,128)(2,1)S(1)}, bf16[128,512]{1,0:T(8,128)(2,1)}, u32[]{:S(2)}) copy-start(bf16[128,512]{1,0:T(8,128)(2,1)} %param.7) | copy-start | bytes 393220
  104.9 48.4 %copy-start.3 = (bf16[128,512]{1,0:T(8,128)(2,1)S(1)}, bf16[128,512]{1,0:T(8,128)(2,1)}, u32[]{:S(2)}) copy-start(bf16[128,512]{1,0:T(8,128)(2,1)} %param.6) | copy-start | bytes 393220
  105.0 48.4 %copy-start.4 = (f32[512]{0:T(512)S(1)}, f32[512]{0:T(512)}, u32[]{:S(2)}) copy-start(f32[512]{0:T(512)} %param.10) | copy-start | bytes 6148
Sparse Core Ops, SparseCore 0:
  155.2 18.6 reduce-scatter.1
where the time goes:
time: 181 us
  waiting for transfers between devices  75 us (41%)
  blocking collectives  46.6 us (26%)
  starting transfers between devices  21.6 us (12%)
  matrix products  17.9 us (10%)
  between operations  13.7 us (8%)
  other arithmetic  4.15 us (2%)
    all_to_all x1, blocking collectives, shards(): lax.all_to_all(turned, 'ctx', split_axis=2, concat_axis=1, tiled=True)  31.8 us
    all_to_all x1, waiting for transfers between devices, shards(): lax.all_to_all(first_section(sent_filter), 'ctx', split_axis=1, concat_ax...  21.2 us
    all_to_all x1, waiting for transfers between devices, shards(): lax.all_to_all(first_section(sent_input), 'ctx', split_axis=1, concat_axi...  20.2 us
    reduce_scatter x1, waiting for transfers between devices, shards(): lax.psum_scatter(lax.dot_general(w_out, gated, (((0,), (1,)), ((), ())),...  18.8 us
    all_to_all x1, blocking collectives, shards(): lax.all_to_all(returned, 'ctx', split_axis=0, concat_axis=1, tiled=True)  14.8 us
    dot_general x12, matrix products, cycle_apply(): return jnp.einsum('kn,zmnc->zmkc', table, operand, precision=precise)  12.8 us
    all_to_all x1, waiting for transfers between devices, shards(): lax.all_to_all(gated_in.reshape(1, ctx_size, per_dev, chan_width), 'ctx',...  7.8 us
    all_to_all x1, starting transfers between devices, shards(): lax.all_to_all(gated_in.reshape(1, ctx_size, per_dev, chan_width), 'ctx',...  7.36 us
  transfers between devices with their start and end apart: 5, of which 5 were waited for; matrix products, arithmetic and copies ran while one was open for 3% of the time, Pallas kernels for 0%

commit v1 on v0

--- a/solution.py
+++ b/solution.py
@@ -5,6 +5,29 @@
 from jax.sharding import PartitionSpec as P
 
 precise = lax.Precision.HIGHEST
+
+
+def in_blocks(shard, dim, size):
+    lengths = shard.shape
+    blocks = shard.reshape(*lengths[:dim], size, lengths[dim] // size, *lengths[dim + 1 :])
+    return jnp.moveaxis(blocks, dim, 0)
+
+
+def joined_along(blocks, dim):
+    blocks = jnp.moveaxis(blocks, 0, dim)
+    lengths = blocks.shape
+    return blocks.reshape(*lengths[:dim], lengths[dim] * lengths[dim + 1], *lengths[dim + 2 :])
+
+
+def swapped_with_each(array, axis, split_dim, concat_dim):
+    peers, mine = (lax.axis_size(axis), lax.axis_index(axis))
+    blocks = in_blocks(array, split_dim, peers)
+    outs = [blocks[mine]]
+    for hop in range(1, peers):
+        sent = blocks[mine ^ hop]
+        outs.append(lax.ppermute(sent, axis, [(i, i ^ hop) for i in range(peers)]))
+    blocks = jnp.stack(outs)[mine ^ jnp.arange(peers)]
+    return joined_along(blocks, concat_dim)
 
 
 def phase_table(row_count, col_count, modulus, factor):
@@ -101,9 +124,7 @@
 
     portion = lax.all_to_all(turned, "ctx", split_axis=2, concat_axis=1, tiled=True)
     returned = last_apply(last_cos, portion[0]) - last_apply(last_sin, portion[1])
-    convolved = lax.all_to_all(returned, "ctx", split_axis=0, concat_axis=1, tiled=True).reshape(
-        tok_rows, chan_width
-    )
+    convolved = swapped_with_each(returned, "ctx", 0, 1).reshape(tok_rows, chan_width)
     gated = (
         query_act.astype(jnp.float32)
         * (convolved + skip_scale[None, :] * gated_in.astype(jnp.float32))

time: 181 us -> 197 us (1.088)
  blocking collectives: 46.6 us -> 0 us
  starting transfers between devices: 21.6 us -> 51.4 us
  waiting for transfers between devices: 75 us -> 103 us
  matrix products: 17.9 us -> 20.1 us
    all_to_all x2 -> x0, blocking collectives: 46.6 us -> none  [the longest x1 31.8 us: shards(): lax.all_to_all(turned, 'ctx', split_axis=2, concat_axis=1, tiled=True)]
    ppermute x0 -> x15, starting transfers between devices: none -> 22.8 us  [swapped_with_each(): outs.append(lax.ppermute(sent, axis, [(i, i ^ hop) for i in range(peers)]))]
    all_to_all x0 -> x1, waiting for transfers between devices: none -> 22.8 us  [shards(): lax.all_to_all(turned, 'ctx', split_axis=2, concat_axis=1, tiled=True)]
    all_to_all x0 -> x1, starting transfers between devices: none -> 7.01 us  [shards(): lax.all_to_all(turned, 'ctx', split_axis=2, concat_axis=1, tiled=True)]
    ppermute x0 -> x15, waiting for transfers between devices: none -> 4.86 us  [swapped_with_each(): outs.append(lax.ppermute(sent, axis, [(i, i ^ hop) for i in range(peers)]))]
    dot_general x1, matrix products: 1.7 us -> 3.89 us  [shards(): lax.dot_general(w_out, gated, (((0,), (1,)), ((), ())), preferred_element...]
  transfers between devices with their start and end apart: 5 -> 21, of which waited for: 5 -> 8; matrix products, arithmetic and copies ran while one was open for 3% -> 3% of each run, Pallas kernels for 0% -> 0%
where the time goes in v1:
time: 197 us; the launch traced here: 196 us
  waiting for transfers between devices  103 us (52%)
  starting transfers between devices  51.4 us (26%)
  matrix products  20.1 us (10%)
  between operations  14 us (7%)
  other arithmetic  4.13 us (2%)
  local copies, waits for them, and re-layouts  3.55 us (2%)
    ppermute x15, starting transfers between devices, swapped_with_each(): outs.append(lax.ppermute(sent, axis, [(i, i ^ hop) for i in range(peers)]))  22.8 us
    all_to_all x1, waiting for transfers between devices, shards(): lax.all_to_all(turned, 'ctx', split_axis=2, concat_axis=1, tiled=True)  22.8 us
    all_to_all x1, waiting for transfers between devices, shards(): lax.all_to_all(first_section(sent_filter), 'ctx', split_axis=1, concat_ax...  21.2 us
    all_to_all x1, waiting for transfers between devices, shards(): lax.all_to_all(first_section(sent_input), 'ctx', split_axis=1, concat_axi...  20.3 us
    reduce_scatter x1, waiting for transfers between devices, shards(): lax.psum_scatter(lax.dot_general(w_out, gated, (((0,), (1,)), ((), ())),...  18.9 us
    dot_general x12, matrix products, cycle_apply(): return jnp.einsum('kn,zmnc->zmkc', table, operand, precision=precise)  12.8 us
    all_to_all x1, waiting for transfers between devices, shards(): lax.all_to_all(gated_in.reshape(1, ctx_size, per_dev, chan_width), 'ctx',...  7.8 us
    all_to_all x1, starting transfers between devices, shards(): lax.all_to_all(gated_in.reshape(1, ctx_size, per_dev, chan_width), 'ctx',...  7.36 us
  transfers between devices with their start and end apart: 21, of which 8 were waited for; matrix products, arithmetic and copies ran while one was open for 3% of the time, Pallas kernels for 0%

profile of v1, /device:TPU:0, one launch (start us, length us, event | category | flops | bytes accessed | tf_op | source)
XLA Modules:
  0.0 195.9 jit_solution(12934322489396149881)
XLA Ops:
  6.5 1.7 fusion.48
  8.2 7.4 %all-to-all-start = ((bf16[1,16,8,512]{3,2,0,1:T(8,128)(2,1)}), bf16[1,16,8,512]{3,2,0,1:T(8,128)(2,1)S(1)}, u32[]{:S(2)}, u32[]{:S(2)}) async-start(bf16[1,16,8,512]{3,2,0,1:T(8,128)(2,1)} %fusion.48), calls=%async_computation | async-start | bytes 262144 | tf_op jit(solution)/shard_map/all_to_all | solution.py:54
  15.7 7.8 %all-to-all-done = bf16[1,16,8,512]{3,2,0,1:T(8,128)(2,1)S(1)} async-done(((bf16[1,16,8,512]{3,2,0,1:T(8,128)(2,1)}), bf16[1,16,8,512]{3,2,0,1:T(8,128)(2,1)S(1)}, u32[]{:S(2)}, u32[]{:S(2)}) %all-to-all-start) | async-done | bytes 131104 | tf_op jit(solution)/shard_map/all_to_all | solution.py:54
  23.5 3.5 %all-to-all-start.2 = ((bf16[1,16,8,512]{3,2,0,1:T(8,128)(2,1)}), bf16[1,16,8,512]{3,2,0,1:T(8,128)(2,1)S(1)}, u32[]{:S(2)}, u32[]{:S(2)}) async-start(bf16[1,16,8,512]{3,2,0,1:T(8,128)(2,1)} %bitcast.245), calls=%async_computation.2 | async-start | bytes 262144 | tf_op jit(solution)/shard_map/all_to_all | solution.py:61
  28.0 6.9 %all-to-all-done.2 = bf16[1,16,8,512]{3,2,0,1:T(8,128)(2,1)S(1)} async-done(((bf16[1,16,8,512]{3,2,0,1:T(8,128)(2,1)}), bf16[1,16,8,512]{3,2,0,1:T(8,128)(2,1)S(1)}, u32[]{:S(2)}, u32[]{:S(2)}) %all-to-all-start.2) | async-done | bytes 131104 | tf_op jit(solution)/shard_map/all_to_all | solution.py:61
  37.8 3.7 %all-to-all-start.3 = ((f32[2,16,2,8,512]{4,3,2,0,1:T(8,128)}), f32[2,16,2,8,512]{4,3,2,0,1:T(8,128)S(1)}, u32[]{:S(2)}, u32[]{:S(2)}) async-start(f32[2,16,2,8,512]{4,3,2,0,1:T(8,128)} %pad_maximum_fusion.1), calls=%async_computation.3 | async-start | bytes 2097152 | tf_op jit(solution)/shard_map/all_to_all | solution.py:92
  43.1 21.2 %all-to-all-done.3 = f32[2,16,2,8,512]{4,3,2,0,1:T(8,128)S(1)} async-done(((f32[2,16,2,8,512]{4,3,2,0,1:T(8,128)}), f32[2,16,2,8,512]{4,3,2,0,1:T(8,128)S(1)}, u32[]{:S(2)}, u32[]{:S(2)}) %all-to-all-start.3) | async-done | bytes 1048608 | tf_op jit(solution)/shard_map/all_to_all | solution.py:92
  64.3 7.0 %all-to-all-start.1 = ((f32[2,16,2,8,512]{4,3,2,0,1:T(8,128)}), f32[2,16,2,8,512]{4,3,2,0,1:T(8,128)S(1)}, u32[]{:S(2)}, u32[]{:S(2)}) async-start(f32[2,16,2,8,512]{4,3,2,0,1:T(8,128)} %pad_maximum_fusion), calls=%async_computation.1 | async-start | bytes 2097152 | tf_op jit(solution)/shard_map/all_to_all | solution.py:89
  71.5 1.1 fusion.15
  72.7 1.1 fusion.14
  73.8 20.3 %all-to-all-done.1 = f32[2,16,2,8,512]{4,3,2,0,1:T(8,128)S(1)} async-done(((f32[2,16,2,8,512]{4,3,2,0,1:T(8,128)}), f32[2,16,2,8,512]{4,3,2,0,1:T(8,128)S(1)}, u32[]{:S(2)}, u32[]{:S(2)}) %all-to-all-start.1) | async-done | bytes 1048608 | tf_op jit(solution)/shard_map/all_to_all | solution.py:89
  94.2 1.1 fusion.13
  95.3 1.1 fusion.12
  96.4 1.1 convolution_subtract_fusion.1
  98.7 1.1 convolution_add_fusion.2
  99.8 1.1 multiply_subtract_fusion
  103.6 1.2 subtract_bitcast_fusion
  106.0 7.0 %all-to-all-start.4 = ((f32[2,2,16,8,512]{4,3,1,0,2:T(8,128)}), f32[2,2,16,8,512]{4,3,1,0,2:T(8,128)S(1)}, u32[]{:S(2)}, u32[]{:S(2)}) async-start(f32[2,2,16,8,512]{4,3,1,0,2:T(8,128)} %copy.79), calls=%async_computation.4 | async-start | bytes 2097152 | tf_op jit(solution)/shard_map/all_to_all | solution.py:125
  113.2 22.8 %all-to-all-done.4 = f32[2,2,16,8,512]{4,3,1,0,2:T(8,128)S(1)} async-done(((f32[2,2,16,8,512]{4,3,1,0,2:T(8,128)}), f32[2,2,16,8,512]{4,3,1,0,2:T(8,128)S(1)}, u32[]{:S(2)}, u32[]{:S(2)}) %all-to-all-start.4) | async-done | bytes 1048608 | tf_op jit(solution)/shard_map/all_to_all | solution.py:125
  138.5 2.0 %collective-permute-start.1 = (f32[1,1,8,512]{3,2,1,0:T(8,128)S(1)}, f32[1,1,8,512]{3,2,1,0:T(8,128)S(1)}, u32[]{:S(2)}, u32[]{:S(2)}) collective-permute-start(f32[1,1,8,512]{3,2,1,0:T(8,128)S(1)} %bitcast.258), channel_id=1, source_target_pairs={{0,4},{2,6},{4,0},{6,2},{8,12},{10,14},{12,8},{14,10},{16,20},{18,... | collective-permute-start | bytes 49160 | tf_op jit(solution)/shard_map/ppermute | solution.py:28
  140.4 2.9 %collective-permute-start.3 = (f32[1,1,8,512]{3,2,1,0:T(8,128)S(1)}, f32[1,1,8,512]{3,2,1,0:T(8,128)S(1)}, u32[]{:S(2)}, u32[]{:S(2)}) collective-permute-start(f32[1,1,8,512]{3,2,1,0:T(8,128)S(1)} %bitcast.254), channel_id=1, source_target_pairs={{0,8},{2,10},{4,12},{6,14},{8,0},{10,2},{12,4},{14,6},{16,24},{18,... | collective-permute-start | bytes 49160 | tf_op jit(solution)/shard_map/ppermute | solution.py:28
  143.7 2.7 %collective-permute-start.5 = (f32[1,1,8,512]{3,2,1,0:T(8,128)S(1)}, f32[1,1,8,512]{3,2,1,0:T(8,128)S(1)}, u32[]{:S(2)}, u32[]{:S(2)}) collective-permute-start(f32[1,1,8,512]{3,2,1,0:T(8,128)S(1)} %bitcast.259), channel_id=1, source_target_pairs={{0,12},{2,14},{4,8},{6,10},{8,4},{10,6},{12,0},{14,2},{16,28},{18,... | collective-permute-start | bytes 49160 | tf_op jit(solution)/shard_map/ppermute | solution.py:28
  146.5 2.9 %collective-permute-start.7 = (f32[1,1,8,512]{3,2,1,0:T(8,128)S(1)}, f32[1,1,8,512]{3,2,1,0:T(8,128)S(1)}, u32[]{:S(2)}, u32[]{:S(2)}) collective-permute-start(f32[1,1,8,512]{3,2,1,0:T(8,128)S(1)} %bitcast.255), channel_id=1, source_target_pairs={{0,16},{2,18},{4,20},{6,22},{8,24},{10,26},{12,28},{14,30},{16,0},... | collective-permute-start | bytes 49160 | tf_op jit(solution)/shard_map/ppermute | solution.py:28
  149.4 2.1 %collective-permute-start.9 = (f32[1,1,8,512]{3,2,1,0:T(8,128)S(1)}, f32[1,1,8,512]{3,2,1,0:T(8,128)S(1)}, u32[]{:S(2)}, u32[]{:S(2)}) collective-permute-start(f32[1,1,8,512]{3,2,1,0:T(8,128)S(1)} %bitcast.251), channel_id=1, source_target_pairs={{0,20},{2,22},{4,16},{6,18},{8,28},{10,30},{12,24},{14,26},{16,4},... | collective-permute-start | bytes 49160 | tf_op jit(solution)/shard_map/ppermute | solution.py:28
  151.5 1.2 collective-permute-start.10
  152.8 2.3 %collective-permute-start.11 = (f32[1,1,8,512]{3,2,1,0:T(8,128)S(1)}, f32[1,1,8,512]{3,2,1,0:T(8,128)S(1)}, u32[]{:S(2)}, u32[]{:S(2)}) collective-permute-start(f32[1,1,8,512]{3,2,1,0:T(8,128)S(1)} %bitcast.249), channel_id=1, source_target_pairs={{0,24},{2,26},{4,28},{6,30},{8,16},{10,18},{12,20},{14,22},{16,8},... | collective-permute-start | bytes 49160 | tf_op jit(solution)/shard_map/ppermute | solution.py:28
  155.1 1.5 collective-permute-start.12
  156.6 3.1 %collective-permute-start.13 = (f32[1,1,8,512]{3,2,1,0:T(8,128)S(1)}, f32[1,1,8,512]{3,2,1,0:T(8,128)S(1)}, u32[]{:S(2)}, u32[]{:S(2)}) collective-permute-start(f32[1,1,8,512]{3,2,1,0:T(8,128)S(1)} %bitcast.247), channel_id=1, source_target_pairs={{0,28},{2,30},{4,24},{6,26},{8,20},{10,22},{12,16},{14,18},{16,12}... | collective-permute-start | bytes 49160 | tf_op jit(solution)/shard_map/ppermute | solution.py:28
  160.8 2.2 %collective-permute-done.13 = f32[1,1,8,512]{3,2,1,0:T(8,128)S(1)} collective-permute-done((f32[1,1,8,512]{3,2,1,0:T(8,128)S(1)}, f32[1,1,8,512]{3,2,1,0:T(8,128)S(1)}, u32[]{:S(2)}, u32[]{:S(2)}) %collective-permute-start.13) | collective-permute-done | bytes 16416 | tf_op jit(solution)/shard_map/ppermute | solution.py:28
  163.1 2.6 %collective-permute-done.14 = f32[1,1,8,512]{3,2,1,0:T(8,128)S(1)} collective-permute-done((f32[1,1,8,512]{3,2,1,0:T(8,128)S(1)}, f32[1,1,8,512]{3,2,1,0:T(8,128)S(1)}, u32[]{:S(2)}, u32[]{:S(2)}) %collective-permute-start.14) | collective-permute-done | bytes 16416 | tf_op jit(solution)/shard_map/ppermute | solution.py:28
  166.3 3.9 %fusion = bf16[4096,128]{0,1:T(8,128)(2,1)} fusion(bf16[512,4096]{1,0:T(8,128)(2,1)} %param.11, f32[16,8,512]{2,1,0:T(8,128)S(1)} %gather_fusion, bf16[128,512]{1,0:T(8,128)(2,1)S(1)} %copy-done.2, f32[512]{0:T(512)S(1)} %copy-done.3, bf16[128,512]{1,0:T(8,128)(2,1)S(1)} %copy-done, bf16[128,512]{1,0:T(8,128)(2,1)S(1)} %copy-done.1), kind=kOutput, calls=%fused_computation.2 | convolution fusion | flops 538050560 | bytes 5900288 | tf_op jit(solution)/shard_map/dot_general | solution.py:133
  170.2 18.9 %reduce-scatter.2.cloned.1.call-done = bf16[2048,128]{0,1:T(8,128)(2,1)} async-done(((bf16[4096,128]{0,1:T(8,128)(2,1)}), bf16[2048,128]{0,1:T(8,128)(2,1)}) %reduce-scatter.2.cloned.1.call-update) | async-done | bytes 524304 | tf_op jit(solution)/shard_map/reduce_scatter | solution.py:132
  (89 shorter events, 15.3 us)
Async XLA Ops:
  8.2 15.3 %all-to-all-start = ((bf16[1,16,8,512]{3,2,0,1:T(8,128)(2,1)}), bf16[1,16,8,512]{3,2,0,1:T(8,128)(2,1)S(1)}, u32[]{:S(2)}, u32[]{:S(2)}) async-start(bf16[1,16,8,512]{3,2,0,1:T(8,128)(2,1)} %fusion.48), calls=%async_computation | async-start | bytes 262144 | tf_op jit(solution)/shard_map/all_to_all | solution.py:54
  23.5 11.4 %all-to-all-start.2 = ((bf16[1,16,8,512]{3,2,0,1:T(8,128)(2,1)}), bf16[1,16,8,512]{3,2,0,1:T(8,128)(2,1)S(1)}, u32[]{:S(2)}, u32[]{:S(2)}) async-start(bf16[1,16,8,512]{3,2,0,1:T(8,128)(2,1)} %bitcast.245), calls=%async_computation.2 | async-start | bytes 262144 | tf_op jit(solution)/shard_map/all_to_all | solution.py:61
  37.8 26.6 %all-to-all-start.3 = ((f32[2,16,2,8,512]{4,3,2,0,1:T(8,128)}), f32[2,16,2,8,512]{4,3,2,0,1:T(8,128)S(1)}, u32[]{:S(2)}, u32[]{:S(2)}) async-start(f32[2,16,2,8,512]{4,3,2,0,1:T(8,128)} %pad_maximum_fusion.1), calls=%async_computation.3 | async-start | bytes 2097152 | tf_op jit(solution)/shard_map/all_to_all | solution.py:92
  64.3 29.8 %all-to-all-start.1 = ((f32[2,16,2,8,512]{4,3,2,0,1:T(8,128)}), f32[2,16,2,8,512]{4,3,2,0,1:T(8,128)S(1)}, u32[]{:S(2)}, u32[]{:S(2)}) async-start(f32[2,16,2,8,512]{4,3,2,0,1:T(8,128)} %pad_maximum_fusion), calls=%async_computation.1 | async-start | bytes 2097152 | tf_op jit(solution)/shard_map/all_to_all | solution.py:89
  106.0 60.2 %copy-start = (bf16[128,512]{1,0:T(8,128)(2,1)S(1)}, bf16[128,512]{1,0:T(8,128)(2,1)}, u32[]{:S(2)}) copy-start(bf16[128,512]{1,0:T(8,128)(2,1)} %param.8) | copy-start | bytes 393220
  106.0 60.3 %copy-start.1 = (bf16[128,512]{1,0:T(8,128)(2,1)S(1)}, bf16[128,512]{1,0:T(8,128)(2,1)}, u32[]{:S(2)}) copy-start(bf16[128,512]{1,0:T(8,128)(2,1)} %param.7) | copy-start | bytes 393220
  106.0 60.3 %copy-start.2 = (bf16[128,512]{1,0:T(8,128)(2,1)S(1)}, bf16[128,512]{1,0:T(8,128)(2,1)}, u32[]{:S(2)}) copy-start(bf16[128,512]{1,0:T(8,128)(2,1)} %param.6) | copy-start | bytes 393220
  106.0 60.3 %copy-start.3 = (f32[512]{0:T(512)S(1)}, f32[512]{0:T(512)}, u32[]{:S(2)}) copy-start(f32[512]{0:T(512)} %param.10) | copy-start | bytes 6148
  106.0 30.0 %all-to-all-start.4 = ((f32[2,2,16,8,512]{4,3,1,0,2:T(8,128)}), f32[2,2,16,8,512]{4,3,1,0,2:T(8,128)S(1)}, u32[]{:S(2)}, u32[]{:S(2)}) async-start(f32[2,2,16,8,512]{4,3,1,0,2:T(8,128)} %copy.79), calls=%async_computation.4 | async-start | bytes 2097152 | tf_op jit(solution)/shard_map/all_to_all | solution.py:125
  113.0 76.1 %reduce-scatter.2.cloned.1.call-start = ((), (), s32[]{:S(2)}) async-start(), calls=%async_computation.6 | async-start | bytes 1572864 | tf_op jit(solution)/shard_map/reduce_scatter | solution.py:132
  137.8 5.9 %collective-permute-start = (f32[1,1,8,512]{3,2,1,0:T(8,128)S(1)}, f32[1,1,8,512]{3,2,1,0:T(8,128)S(1)}, u32[]{:S(2)}, u32[]{:S(2)}) collective-permute-start(f32[1,1,8,512]{3,2,1,0:T(8,128)S(1)} %bitcast.260), channel_id=1, source_target_pairs={{0,2},{2,0},{4,6},{6,4},{8,10},{10,8},{12,14},{14,12},{16,18},{18,... | collective-permute-start | bytes 49160 | tf_op jit(solution)/shard_map/ppermute | solution.py:28
  138.5 8.0 %collective-permute-start.1 = (f32[1,1,8,512]{3,2,1,0:T(8,128)S(1)}, f32[1,1,8,512]{3,2,1,0:T(8,128)S(1)}, u32[]{:S(2)}, u32[]{:S(2)}) collective-permute-start(f32[1,1,8,512]{3,2,1,0:T(8,128)S(1)} %bitcast.258), channel_id=1, source_target_pairs={{0,4},{2,6},{4,0},{6,2},{8,12},{10,14},{12,8},{14,10},{16,20},{18,... | collective-permute-start | bytes 49160 | tf_op jit(solution)/shard_map/ppermute | solution.py:28
  140.4 6.0 %collective-permute-start.2 = (f32[1,1,8,512]{3,2,1,0:T(8,128)S(1)}, f32[1,1,8,512]{3,2,1,0:T(8,128)S(1)}, u32[]{:S(2)}, u32[]{:S(2)}) collective-permute-start(f32[1,1,8,512]{3,2,1,0:T(8,128)S(1)} %bitcast.256), channel_id=1, source_target_pairs={{0,6},{2,4},{4,2},{6,0},{8,14},{10,12},{12,10},{14,8},{16,22},{18,... | collective-permute-start | bytes 49160 | tf_op jit(solution)/shard_map/ppermute | solution.py:28
  140.4 9.0 %collective-permute-start.3 = (f32[1,1,8,512]{3,2,1,0:T(8,128)S(1)}, f32[1,1,8,512]{3,2,1,0:T(8,128)S(1)}, u32[]{:S(2)}, u32[]{:S(2)}) collective-permute-start(f32[1,1,8,512]{3,2,1,0:T(8,128)S(1)} %bitcast.254), channel_id=1, source_target_pairs={{0,8},{2,10},{4,12},{6,14},{8,0},{10,2},{12,4},{14,6},{16,24},{18,... | collective-permute-start | bytes 49160 | tf_op jit(solution)/shard_map/ppermute | solution.py:28
  143.3 6.1 %collective-permute-start.4 = (f32[1,1,8,512]{3,2,1,0:T(8,128)S(1)}, f32[1,1,8,512]{3,2,1,0:T(8,128)S(1)}, u32[]{:S(2)}, u32[]{:S(2)}) collective-permute-start(f32[1,1,8,512]{3,2,1,0:T(8,128)S(1)} %bitcast.252), channel_id=1, source_target_pairs={{0,10},{2,8},{4,14},{6,12},{8,2},{10,0},{12,6},{14,4},{16,26},{18,... | collective-permute-start | bytes 49160 | tf_op jit(solution)/shard_map/ppermute | solution.py:28
  143.7 7.8 %collective-permute-start.5 = (f32[1,1,8,512]{3,2,1,0:T(8,128)S(1)}, f32[1,1,8,512]{3,2,1,0:T(8,128)S(1)}, u32[]{:S(2)}, u32[]{:S(2)}) collective-permute-start(f32[1,1,8,512]{3,2,1,0:T(8,128)S(1)} %bitcast.259), channel_id=1, source_target_pairs={{0,12},{2,14},{4,8},{6,10},{8,4},{10,6},{12,0},{14,2},{16,28},{18,... | collective-permute-start | bytes 49160 | tf_op jit(solution)/shard_map/ppermute | solution.py:28
  146.4 6.3 %collective-permute-start.6 = (f32[1,1,8,512]{3,2,1,0:T(8,128)S(1)}, f32[1,1,8,512]{3,2,1,0:T(8,128)S(1)}, u32[]{:S(2)}, u32[]{:S(2)}) collective-permute-start(f32[1,1,8,512]{3,2,1,0:T(8,128)S(1)} %bitcast.257), channel_id=1, source_target_pairs={{0,14},{2,12},{4,10},{6,8},{8,6},{10,4},{12,2},{14,0},{16,30},{18,... | collective-permute-start | bytes 49160 | tf_op jit(solution)/shard_map/ppermute | solution.py:28
  146.5 8.6 %collective-permute-start.7 = (f32[1,1,8,512]{3,2,1,0:T(8,128)S(1)}, f32[1,1,8,512]{3,2,1,0:T(8,128)S(1)}, u32[]{:S(2)}, u32[]{:S(2)}) collective-permute-start(f32[1,1,8,512]{3,2,1,0:T(8,128)S(1)} %bitcast.255), channel_id=1, source_target_pairs={{0,16},{2,18},{4,20},{6,22},{8,24},{10,26},{12,28},{14,30},{16,0},... | collective-permute-start | bytes 49160 | tf_op jit(solution)/shard_map/ppermute | solution.py:28
  149.4 7.2 %collective-permute-start.8 = (f32[1,1,8,512]{3,2,1,0:T(8,128)S(1)}, f32[1,1,8,512]{3,2,1,0:T(8,128)S(1)}, u32[]{:S(2)}, u32[]{:S(2)}) collective-permute-start(f32[1,1,8,512]{3,2,1,0:T(8,128)S(1)} %bitcast.253), channel_id=1, source_target_pairs={{0,18},{2,16},{4,22},{6,20},{8,26},{10,24},{12,30},{14,28},{16,2},... | collective-permute-start | bytes 49160 | tf_op jit(solution)/shard_map/ppermute | solution.py:28
  149.4 10.3 %collective-permute-start.9 = (f32[1,1,8,512]{3,2,1,0:T(8,128)S(1)}, f32[1,1,8,512]{3,2,1,0:T(8,128)S(1)}, u32[]{:S(2)}, u32[]{:S(2)}) collective-permute-start(f32[1,1,8,512]{3,2,1,0:T(8,128)S(1)} %bitcast.251), channel_id=1, source_target_pairs={{0,20},{2,22},{4,16},{6,18},{8,28},{10,30},{12,24},{14,26},{16,4},... | collective-permute-start | bytes 49160 | tf_op jit(solution)/shard_map/ppermute | solution.py:28
  151.5 9.2 %collective-permute-start.10 = (f32[1,1,8,512]{3,2,1,0:T(8,128)S(1)}, f32[1,1,8,512]{3,2,1,0:T(8,128)S(1)}, u32[]{:S(2)}, u32[]{:S(2)}) collective-permute-start(f32[1,1,8,512]{3,2,1,0:T(8,128)S(1)} %bitcast.250), channel_id=1, source_target_pairs={{0,22},{2,20},{4,18},{6,16},{8,30},{10,28},{12,26},{14,24},{16,6},... | collective-permute-start | bytes 49160 | tf_op jit(solution)/shard_map/ppermute | solution.py:28
  152.8 8.0 %collective-permute-start.11 = (f32[1,1,8,512]{3,2,1,0:T(8,128)S(1)}, f32[1,1,8,512]{3,2,1,0:T(8,128)S(1)}, u32[]{:S(2)}, u32[]{:S(2)}) collective-permute-start(f32[1,1,8,512]{3,2,1,0:T(8,128)S(1)} %bitcast.249), channel_id=1, source_target_pairs={{0,24},{2,26},{4,28},{6,30},{8,16},{10,18},{12,20},{14,22},{16,8},... | collective-permute-start | bytes 49160 | tf_op jit(solution)/shard_map/ppermute | solution.py:28
  155.1 5.7 %collective-permute-start.12 = (f32[1,1,8,512]{3,2,1,0:T(8,128)S(1)}, f32[1,1,8,512]{3,2,1,0:T(8,128)S(1)}, u32[]{:S(2)}, u32[]{:S(2)}) collective-permute-start(f32[1,1,8,512]{3,2,1,0:T(8,128)S(1)} %bitcast.248), channel_id=1, source_target_pairs={{0,26},{2,24},{4,30},{6,28},{8,18},{10,16},{12,22},{14,20},{16,10}... | collective-permute-start | bytes 49160 | tf_op jit(solution)/shard_map/ppermute | solution.py:28
  156.6 6.4 %collective-permute-start.13 = (f32[1,1,8,512]{3,2,1,0:T(8,128)S(1)}, f32[1,1,8,512]{3,2,1,0:T(8,128)S(1)}, u32[]{:S(2)}, u32[]{:S(2)}) collective-permute-start(f32[1,1,8,512]{3,2,1,0:T(8,128)S(1)} %bitcast.247), channel_id=1, source_target_pairs={{0,28},{2,30},{4,24},{6,26},{8,20},{10,22},{12,16},{14,18},{16,12}... | collective-permute-start | bytes 49160 | tf_op jit(solution)/shard_map/ppermute | solution.py:28
  159.7 5.9 %collective-permute-start.14 = (f32[1,1,8,512]{3,2,1,0:T(8,128)S(1)}, f32[1,1,8,512]{3,2,1,0:T(8,128)S(1)}, u32[]{:S(2)}, u32[]{:S(2)}) collective-permute-start(f32[1,1,8,512]{3,2,1,0:T(8,128)S(1)} %bitcast.246), channel_id=1, source_target_pairs={{0,30},{2,28},{4,26},{6,24},{8,22},{10,20},{12,18},{14,16},{16,14}... | collective-permute-start | bytes 49160 | tf_op jit(solution)/shard_map/ppermute | solution.py:28
Sparse Core Ops, SparseCore 0:
  170.3 18.7 reduce-scatter.1
